TPU v7x, 256 devices: a whole 4x4x8 slice. The times are simulated.
256 devices in a mesh: req: 8 (over z_hi, x), tile: 16 (over z_lo, y), tp: 2 (over core).
Axes of the slice: x: 4, y: 4, z: 8 (z_hi: 2, z_lo: 4; z = z_hi * 4 + z_lo), core: 2. Of those that a mesh axis runs over, the one named last changes fastest.
Arguments:
- image_qkv: bfloat16 [128, 144, 3, 2048], P(('req', 'tile'), None, None, 'tp'), parts along dimension 0, may hold values from -6 to 6
- text_kv: bfloat16 [4096, 2, 2048], P(('req', 'tile'), None, 'tp'), parts along dimension 0, may hold values from -6 to 6
- q_gain: float32 [128], replicated, may hold values from 0.7 to 5
- k_gain: float32 [128], replicated, may hold values from 0.7 to 5
- out_weight: bfloat16 [2048, 3072], P('tp'), may hold values from -0.125 to 0.125
- hidden: bfloat16 [128, 144, 3072], P(('req', 'tile')), parts along dimension 0, may hold values from -6 to 6
- mlp_term: bfloat16 [128, 144, 3072], P(('req', 'tile')), parts along dimension 0, may hold values from -3 to 3
- gate: float32 [24576], P('req'), parts along dimension 0, may hold values from -4 to 4
- final_shift: float32 [24576], P('req'), parts along dimension 0, may hold values from -3 to 3
- final_scale: float32 [24576], P('req'), parts along dimension 0, may hold values from -3 to 3
- final_weight: bfloat16 [3072, 64], replicated, may hold values from -0.109375 to 0.109375
- final_bias: float32 [64], replicated, may hold values from -3 to 3
- latent: float32 [128, 144, 64], P(('req', 'tile')), parts along dimension 0, may hold values from -6 to 6
- image_size: int32 [16], P('req'), parts along dimension 0, may hold values from 24 to 48, as said below
- text_len: int32 [8], P('req'), parts along dimension 0, may hold values from 64 to 512
- timestep: int32 [8], P('req'), parts along dimension 0, may hold values from 0 to 27
Outputs:
- velocity: float32 [128, 144, 64], P(('req', 'tile')), parts along dimension 0
- latent_next: float32 [128, 144, 64], P(('req', 'tile')), parts along dimension 0
There are 8 independent parts, one for each index of `req`. A program takes and returns all parts, laid end to end along the dimension named above; an argument that names none is the same for every part. Nothing has to cross between parts.
Inputs may be any that keep to these rules, and one draw needn't show every extreme that they name: The larger of image_size[0] and image_size[1] equals 48.
All inputs are finite; a program needn't handle non-finite values.
Results may differ from a plain program's by a relative error of at most 0.014.
The roundings to bfloat16 on the way count: a program that leaves them out, or rounds other values in their place, can miss the bound.
Values may be sent and summed in bfloat16 or wider, within the bound.
No kernel may reach another device: no remote copies, remote signals or barrier semaphores. Data moves between devices by JAX's collectives and lax.ppermute only.
A program may use at most 128 MiB of HBM per device.

v0:
```python
import jax
import jax.numpy as jnp
from jax import lax
from jax.sharding import PartitionSpec as P

HEAD = 128
STEPS = 28
CANVAS = 48


def angle_table(row_pos, col_pos, head_size):
    first_part = head_size // 8
    side_dims = (head_size - first_part) // 2
    side_index = jnp.arange(side_dims // 2, dtype=jnp.float32)
    frequency = jnp.power(10000.0, -2.0 * side_index / side_dims)
    still = jnp.zeros(row_pos.shape + (first_part // 2,), jnp.float32)
    return jnp.concatenate(
        [still, row_pos[..., None] * frequency, col_pos[..., None] * frequency], axis=-1
    )


def norm_rope(vectors, gain_vector, angles):
    values_wide = vectors.astype(jnp.float32)
    scaled = (
        values_wide
        * lax.rsqrt(jnp.mean(values_wide * values_wide, axis=-1, keepdims=True) + 1e-06)
        * gain_vector
    )
    paired = scaled.reshape(scaled.shape[:-1] + (scaled.shape[-1] // 2, 2))
    cosine = jnp.cos(angles)[:, None, :]
    sine = jnp.sin(angles)[:, None, :]
    first_part = paired[..., 0]
    second_part = paired[..., 1]
    rotated = jnp.stack(
        [first_part * cosine - second_part * sine, first_part * sine + second_part * cosine],
        axis=-1,
    )
    return rotated.reshape(scaled.shape).astype(jnp.bfloat16)


def euler_step(image_size, timestep):
    area = (image_size[0] * image_size[1]).astype(jnp.float32)
    shift_factor = jnp.exp(0.5 + 0.65 * (area - 256.0) / 3840.0)
    now_time = 1.0 - timestep[0].astype(jnp.float32) / STEPS
    next_time = 1.0 - (timestep[0] + 1).astype(jnp.float32) / STEPS

    def sigma_of(moment):
        return shift_factor * moment / (shift_factor * moment + 1.0 - moment)

    return sigma_of(next_time) - sigma_of(now_time)


def grid_position(tile_number, local_index, grid_x, tile_h, tile_w):
    row_pos = tile_number // grid_x * tile_h + local_index // tile_w
    col_pos = tile_number % grid_x * tile_w + local_index % tile_w
    return (row_pos, col_pos)


def attend_block(state_carry, query_block, piece_keys, piece_values, key_mask):
    running_max, totals, blended = state_carry
    scale_factor = query_block.shape[-1] ** (-0.5)
    scores = (
        jnp.einsum("hqd,khd->hqk", query_block, piece_keys, preferred_element_type=jnp.float32)
        * scale_factor
    )
    scores = jnp.where(key_mask[None, None, :], scores, -jnp.inf)
    new_max = jnp.max(scores, axis=2)
    safe_max = jnp.where(new_max == -jnp.inf, 0.0, new_max)
    factor = jnp.exp(running_max - safe_max)
    weights = jnp.exp(scores - safe_max[..., None])
    totals = totals * factor + jnp.sum(weights, axis=2)
    blended = blended * factor[..., None] + jnp.einsum(
        "hqk,khd->hqd",
        weights.astype(jnp.bfloat16),
        piece_values,
        preferred_element_type=jnp.float32,
    )
    return (new_max, totals, blended)


def guarded(active, state_carry, query_block, piece_keys, piece_values, key_mask):

    def compute(inner_state):
        return attend_block(inner_state, query_block, piece_keys, piece_values, key_mask)

    def unchanged(inner_state):
        return inner_state

    return lax.cond(active, compute, unchanged, state_carry)


def shards(
    image_qkv,
    text_kv,
    q_gain,
    k_gain,
    out_weight,
    hidden,
    mlp_term,
    gate,
    final_shift,
    final_scale,
    final_weight,
    final_bias,
    latent,
    image_size,
    text_len,
    timestep,
):
    tile_count = lax.axis_size("tile")
    grid_x = min(tile_count, 4)
    grid_y = tile_count // grid_x
    tile_w = CANVAS // grid_x
    tile_h = CANVAS // grid_y
    pixels = tile_h * tile_w
    head_size = HEAD
    feature_width = image_qkv.shape[3]
    head_count = feature_width // head_size
    text_rows = text_kv.shape[0]
    model_width = hidden.shape[2]
    latent_width = final_weight.shape[1]
    tile_index = lax.axis_index("tile")
    local_index = jnp.arange(pixels, dtype=jnp.int32)
    row_pos, col_pos = grid_position(tile_index, local_index, grid_x, tile_h, tile_w)
    patch_live = (row_pos < image_size[0]) & (col_pos < image_size[1])
    angles = angle_table(row_pos.astype(jnp.float32), col_pos.astype(jnp.float32), head_size)
    triple = image_qkv.reshape(pixels, 3, head_count, head_size)
    text_pair = text_kv.reshape(text_rows, 2, head_count, head_size)
    own_query = norm_rope(triple[:, 0], q_gain, angles)
    text_keys = norm_rope(
        text_pair[:, 0], k_gain, jnp.zeros((text_rows, head_size // 2), jnp.float32)
    )
    block_keys = jnp.concatenate([norm_rope(triple[:, 1], k_gain, angles), text_keys], axis=0)
    block_values = jnp.concatenate([triple[:, 2], text_pair[:, 1]], axis=0)
    key_rows = pixels + text_rows
    query_live = (row_pos < image_size[0]) & (col_pos < image_size[1])
    query_heads = own_query.transpose(1, 0, 2)
    block_rows = pixels // 4
    piece_keys = lax.all_gather(block_keys, "tile", axis=0, tiled=True)
    piece_values = lax.all_gather(block_values, "tile", axis=0, tiled=True)
    index = jnp.arange(piece_keys.shape[0], dtype=jnp.int32)
    source = index // key_rows
    within = index % key_rows
    key_row, key_col = grid_position(source, within, grid_x, tile_h, tile_w)
    image_ok = (within < pixels) & (key_row < image_size[0]) & (key_col < image_size[1])
    slot = source * text_rows + within - pixels
    text_ok = (within >= pixels) & (slot < text_len[0])
    key_mask = image_ok | text_ok
    any_key = jnp.any(key_mask)
    running_max = jnp.full((head_count, pixels), -jnp.inf, jnp.float32)
    totals = jnp.zeros((head_count, pixels), jnp.float32)
    blended = jnp.zeros((head_count, pixels, head_size), jnp.float32)
    parts_max = []
    parts_total = []
    parts_blend = []
    for block_index in range(4):
        row_start = block_index * block_rows
        row_stop = row_start + block_rows
        active = any_key & jnp.any(query_live[row_start:row_stop])
        piece_state = (
            running_max[:, row_start:row_stop],
            totals[:, row_start:row_stop],
            blended[:, row_start:row_stop],
        )
        new_max, new_total, new_blend = guarded(
            active,
            piece_state,
            query_heads[:, row_start:row_stop],
            piece_keys,
            piece_values,
            key_mask,
        )
        parts_max.append(new_max)
        parts_total.append(new_total)
        parts_blend.append(new_blend)
    totals = jnp.concatenate(parts_total, axis=1)
    blended = jnp.concatenate(parts_blend, axis=1)
    safe_total = jnp.where(totals > 0, totals, 1.0)
    result = jnp.where(totals[..., None] > 0, blended / safe_total[..., None], 0.0)
    result = result.transpose(1, 0, 2).reshape(pixels, feature_width).astype(jnp.bfloat16)
    projected = lax.psum(
        jnp.dot(result, out_weight, preferred_element_type=jnp.float32).astype(jnp.bfloat16), "tp"
    ).astype(jnp.float32)
    state = hidden.reshape(pixels, model_width).astype(jnp.float32) + gate * (
        projected + mlp_term.reshape(pixels, model_width).astype(jnp.float32)
    )
    centered = state - jnp.mean(state, axis=-1, keepdims=True)
    normed = centered * lax.rsqrt(jnp.mean(centered * centered, axis=-1, keepdims=True) + 1e-06)
    modulated = (normed * (1.0 + final_scale) + final_shift).astype(jnp.bfloat16)
    velocity = jnp.dot(modulated, final_weight, preferred_element_type=jnp.float32) + final_bias
    velocity = jnp.where(patch_live[:, None], velocity, 0.0)
    latent_next = latent.reshape(pixels, latent_width) + euler_step(image_size, timestep) * velocity
    return (velocity.reshape(1, pixels, latent_width), latent_next.reshape(1, pixels, latent_width))


def solution(mesh):
    placed = (
        P(("req", "tile"), None, None, "tp"),
        P(("req", "tile"), None, "tp"),
        P(),
        P(),
        P("tp", None),
        P(("req", "tile"), None, None),
        P(("req", "tile"), None, None),
        P("req"),
        P("req"),
        P("req"),
        P(),
        P(),
        P(("req", "tile"), None, None),
        P("req"),
        P("req"),
        P("req"),
    )
    return jax.shard_map(
        shards,
        mesh=mesh,
        in_specs=placed,
        out_specs=(P(("req", "tile"), None, None), P(("req", "tile"), None, None)),
        check_vma=False,
    )
```

profile of v0, /device:TPU:1, one launch (start us, length us, event | category | flops | bytes accessed | tf_op | source)
XLA Modules:
  0.0 287.4 jit_solution(2902120326532575079)
XLA Ops:
  7.3 1.4 copy.81
  8.8 1.0 multiply_reduce_fusion.1
  16.1 1.2 copy.63
  19.4 1.9 fusion.131
  21.3 1.2 compare_and_fusion
  28.0 1.2 fusion.121
  29.4 76.1 %all-gather.3.cloned.1.call-done = bf16[2816,8,128]{2,1,0:T(8,128)(2,1)} async-done(((bf16[176,8,128]{2,1,0:T(8,128)(2,1)}), bf16[2816,8,128]{2,1,0:T(8,128)(2,1)}) %all-gather.3.cloned.1.call-update) | async-done | bytes 5767184 | tf_op jit(solution)/shard_map/all_gather | solution.py:139
  105.4 91.0 %all-gather.5.cloned.1.call-done = bf16[2816,8,128]{2,1,0:T(8,128)(2,1)} async-done(((bf16[176,8,128]{2,1,0:T(8,128)(2,1)}), bf16[2816,8,128]{2,1,0:T(8,128)(2,1)}) %all-gather.5.cloned.1.call-update) | async-done | bytes 5767184 | tf_op jit(solution)/shard_map/all_gather | solution.py:140
  196.5 9.6 %conditional.4 = (f32[8,36,128]{2,1,0:T(8,128)S(1)}, f32[8,36]{1,0:T(8,128)S(1)}) conditional(s32[]{:T(128)} %convert_element_type.123, () %tuple.56, (pred[2816]{0:T(1024)(128)(4,1)S(1)}, bf16[8,144,128]{1,0,2:T(8,128)(2,1)S(1)}, bf16[2816,8,128]{2,1,0:T(8,128)(2,1)}, bf16[2816,8,128]{2,1,0:T(8,128)(2,1)}) %tuple.113), branch_computations={%region_5.6_spmd, %region_6.9_spmd} | conditional | flops 420951456 | bytes 39402944 | solution.py:89
  196.9 6.4 %fusion.132 = (f32[8,36]{1,0:T(8,128)S(1)}, f32[8,36,2816]{2,1,0:T(8,128)S(1)}) fusion(bf16[2816,8,128]{2,1,0:T(8,128)(2,1)} %get-tuple-element.112, bf16[8,144,128]{2,1,0:T(8,128)(2,1)S(1)} %copy.64, pred[2816]{0:T(1024)(128)(4,1)S(1)} %get-tuple-element.44), kind=kOutput, calls=%fused_computation.174 | convolution fusion | flops 210050784 | bytes 9097344 | tf_op jit(solution)/shard_map/cond/branch_1_fun/hqd,khd->hqk/dot_general | solution.py:63
  204.0 2.1 fusion.14
  206.1 9.8 %conditional.5 = (f32[8,36,128]{2,1,0:T(8,128)S(1)}, f32[8,36]{1,0:T(8,128)S(1)}) conditional(s32[]{:T(128)} %convert_element_type.138, () %tuple.58, (pred[2816]{0:T(1024)(128)(4,1)S(1)}, bf16[8,144,128]{1,0,2:T(8,128)(2,1)S(1)}, bf16[2816,8,128]{2,1,0:T(8,128)(2,1)}, bf16[2816,8,128]{2,1,0:T(8,128)(2,1)}) %tuple.114), branch_computations={%region_10.11_spmd, %region_11.14_spmd} | conditional | flops 420951456 | bytes 39402944 | solution.py:89
  206.7 6.4 %fusion.133 = (f32[8,36]{1,0:T(8,128)S(1)}, f32[8,36,2816]{2,1,0:T(8,128)S(1)}) fusion(bf16[2816,8,128]{2,1,0:T(8,128)(2,1)} %get-tuple-element.116, bf16[8,144,128]{2,1,0:T(8,128)(2,1)S(1)} %copy.67, pred[2816]{0:T(1024)(128)(4,1)S(1)} %get-tuple-element.48), kind=kOutput, calls=%fused_computation.175 | convolution fusion | flops 210050784 | bytes 9097344 | tf_op jit(solution)/shard_map/cond/branch_1_fun/hqd,khd->hqk/dot_general | solution.py:63
  213.8 2.1 fusion.35
  215.9 9.6 %conditional.6 = (f32[8,36,128]{2,1,0:T(8,128)S(1)}, f32[8,36]{1,0:T(8,128)S(1)}) conditional(s32[]{:T(128)} %convert_element_type.139, () %tuple.59, (pred[2816]{0:T(1024)(128)(4,1)S(1)}, bf16[8,144,128]{1,0,2:T(8,128)(2,1)S(1)}, bf16[2816,8,128]{2,1,0:T(8,128)(2,1)}, bf16[2816,8,128]{2,1,0:T(8,128)(2,1)}) %tuple.115), branch_computations={%region_15.16_spmd, %region_16.19_spmd} | conditional | flops 420951456 | bytes 39402944 | solution.py:89
  216.4 6.4 %fusion.134 = (f32[8,36]{1,0:T(8,128)S(1)}, f32[8,36,2816]{2,1,0:T(8,128)S(1)}) fusion(bf16[2816,8,128]{2,1,0:T(8,128)(2,1)} %get-tuple-element.120, bf16[8,144,128]{2,1,0:T(8,128)(2,1)S(1)} %copy.70, pred[2816]{0:T(1024)(128)(4,1)S(1)} %get-tuple-element.52), kind=kOutput, calls=%fused_computation.176 | convolution fusion | flops 210050784 | bytes 9097344 | tf_op jit(solution)/shard_map/cond/branch_1_fun/hqd,khd->hqk/dot_general | solution.py:63
  223.4 2.1 fusion.56
  225.5 9.8 %conditional.7 = (f32[8,36,128]{2,1,0:T(8,128)S(1)}, f32[8,36]{1,0:T(8,128)S(1)}) conditional(s32[]{:T(128)} %convert_element_type.140, () %tuple.60, (pred[2816]{0:T(1024)(128)(4,1)S(1)}, bf16[8,144,128]{1,0,2:T(8,128)(2,1)S(1)}, bf16[2816,8,128]{2,1,0:T(8,128)(2,1)}, bf16[2816,8,128]{2,1,0:T(8,128)(2,1)}) %tuple.116), branch_computations={%region_20.21_spmd, %region_21.24_spmd} | conditional | flops 420951456 | bytes 39402944 | solution.py:89
  226.2 6.4 %fusion.135 = (f32[8,36]{1,0:T(8,128)S(1)}, f32[8,36,2816]{2,1,0:T(8,128)S(1)}) fusion(bf16[2816,8,128]{2,1,0:T(8,128)(2,1)} %get-tuple-element.124, bf16[8,144,128]{2,1,0:T(8,128)(2,1)S(1)} %copy.73, pred[2816]{0:T(1024)(128)(4,1)S(1)} %get-tuple-element.56), kind=kOutput, calls=%fused_computation.177 | convolution fusion | flops 210050784 | bytes 9097344 | tf_op jit(solution)/shard_map/cond/branch_1_fun/hqd,khd->hqk/dot_general | solution.py:63
  233.3 2.1 fusion.77
  235.6 5.1 %convolution_convert_fusion = bf16[144,3072]{1,0:T(8,128)(2,1)} fusion(bf16[1024,3072]{1,0:T(8,128)(2,1)} %param.28, f32[8,144]{1,0:T(8,128)S(1)} %broadcast_select_fusion, f32[8,36,128]{2,1,0:T(8,128)S(1)} %get-tuple-element.77, f32[8,36,128]{2,1,0:T(8,128)S(1)} %get-tuple-element.76, f32[8,36,128]{2,1,0:T(8,128)S(1)} %get-tuple-element.75, ...), kind=kOutput, calls=%fused_computation.60 | convolution fusion | flops 907296768 | bytes 7771776 | tf_op jit(solution)/shard_map/dot_general | solution.py:182
  242.7 33.1 %all-reduce.2.cloned.1.call-done = bf16[144,3072]{1,0:T(8,128)(2,1)} async-done(((bf16[144,3072]{1,0:T(8,128)(2,1)}), bf16[144,3072]{1,0:T(8,128)(2,1)}) %all-reduce.2.cloned.1.call-update) | async-done | bytes 884752 | tf_op jit(solution)/shard_map/psum | solution.py:181
  275.8 1.7 fusion.96
  277.6 1.8 multiply_reduce_fusion
  (111 shorter events, 14.5 us)
Async XLA Ops:
  7.2 272.2 %copy-start = (bf16[3072,64]{0,1:T(8,128)(2,1)S(1)}, bf16[3072,64]{0,1:T(8,128)(2,1)}, u32[]{:S(2)}) copy-start(bf16[3072,64]{0,1:T(8,128)(2,1)} %param.34) | copy-start | bytes 1179652
  7.2 2.6 copy-start.5
  7.2 98.3 %all-gather.3.cloned.1.call-start = ((), (), s32[]{:S(2)}) async-start(), calls=%async_computation | async-start | bytes 6127616 | tf_op jit(solution)/shard_map/all_gather | solution.py:139
  8.7 4.9 %copy-start.11 = (f32[128]{0:T(128)S(1)}, f32[128]{0:T(128)}, u32[]{:S(2)}) copy-start(f32[128]{0:T(128)} %param.27) | copy-start | bytes 1540
  8.7 5.1 %copy-start.12 = (f32[128]{0:T(128)S(1)}, f32[128]{0:T(128)}, u32[]{:S(2)}) copy-start(f32[128]{0:T(128)} %param.26) | copy-start | bytes 1540
  15.3 3.5 %copy-start.10 = (s32[2]{0:T(128)S(1)}, s32[2]{0:T(128)}, u32[]{:S(2)}) copy-start(s32[2]{0:T(128)} %param.37) | copy-start | bytes 28
  17.3 179.2 %all-gather.5.cloned.1.call-start = ((), (), s32[]{:S(2)}) async-start(), calls=%async_computation.1 | async-start | bytes 6127616 | tf_op jit(solution)/shard_map/all_gather | solution.py:140
  18.2 257.7 %all-reduce.2.cloned.1.call-start = ((), (), s32[]{:S(2)}) async-start(), calls=%async_computation.2 | async-start | bytes 1769472 | tf_op jit(solution)/shard_map/psum | solution.py:181
  196.9 7.1 %slice-start = ((s8[5767168]{0:T(1024)(128)(4,1)}), s8[4194304]{0:T(1024)(128)(4,1)S(1)}, s32[]{:S(2)}) async-start(s8[5767168]{0:T(1024)(128)(4,1)} %bitcast.71), calls=%async_computation.3 | async-start | bytes 8388608 | tf_op jit(solution)/shard_map/cond
  196.9 7.1 %slice-start.1 = ((s8[5767168]{0:T(1024)(128)(4,1)}), s8[1572864]{0:T(1024)(128)(4,1)S(1)}, s32[]{:S(2)}) async-start(s8[5767168]{0:T(1024)(128)(4,1)} %bitcast.71), calls=%async_computation.4 | async-start | bytes 3145728 | tf_op jit(solution)/shard_map/cond
  206.7 7.1 %slice-start.2 = ((s8[5767168]{0:T(1024)(128)(4,1)}), s8[4194304]{0:T(1024)(128)(4,1)S(1)}, s32[]{:S(2)}) async-start(s8[5767168]{0:T(1024)(128)(4,1)} %bitcast.73), calls=%async_computation.5 | async-start | bytes 8388608 | tf_op jit(solution)/shard_map/cond
  206.7 7.1 %slice-start.3 = ((s8[5767168]{0:T(1024)(128)(4,1)}), s8[1572864]{0:T(1024)(128)(4,1)S(1)}, s32[]{:S(2)}) async-start(s8[5767168]{0:T(1024)(128)(4,1)} %bitcast.73), calls=%async_computation.6 | async-start | bytes 3145728 | tf_op jit(solution)/shard_map/cond
  216.3 7.1 %slice-start.4 = ((s8[5767168]{0:T(1024)(128)(4,1)}), s8[4194304]{0:T(1024)(128)(4,1)S(1)}, s32[]{:S(2)}) async-start(s8[5767168]{0:T(1024)(128)(4,1)} %bitcast.75), calls=%async_computation.7 | async-start | bytes 8388608 | tf_op jit(solution)/shard_map/cond
  216.3 7.1 %slice-start.5 = ((s8[5767168]{0:T(1024)(128)(4,1)}), s8[1572864]{0:T(1024)(128)(4,1)S(1)}, s32[]{:S(2)}) async-start(s8[5767168]{0:T(1024)(128)(4,1)} %bitcast.75), calls=%async_computation.8 | async-start | bytes 3145728 | tf_op jit(solution)/shard_map/cond
  226.2 7.1 %slice-start.6 = ((s8[5767168]{0:T(1024)(128)(4,1)}), s8[4194304]{0:T(1024)(128)(4,1)S(1)}, s32[]{:S(2)}) async-start(s8[5767168]{0:T(1024)(128)(4,1)} %bitcast.77), calls=%async_computation.9 | async-start | bytes 8388608 | tf_op jit(solution)/shard_map/cond
  226.2 7.1 %slice-start.7 = ((s8[5767168]{0:T(1024)(128)(4,1)}), s8[1572864]{0:T(1024)(128)(4,1)S(1)}, s32[]{:S(2)}) async-start(s8[5767168]{0:T(1024)(128)(4,1)} %bitcast.77), calls=%async_computation.10 | async-start | bytes 3145728 | tf_op jit(solution)/shard_map/cond
  235.5 7.2 %copy-start.9 = (f32[3072]{0:T(1024)S(1)}, f32[3072]{0:T(1024)}, u32[]{:S(2)}) copy-start(f32[3072]{0:T(1024)} %param.33) | copy-start | bytes 36868
  235.5 40.3 %copy-start.1 = (bf16[1,144,3072]{2,1,0:T(8,128)(2,1)S(1)}, bf16[1,144,3072]{2,1,0:T(8,128)(2,1)}, u32[]{:S(2)}) copy-start(bf16[1,144,3072]{2,1,0:T(8,128)(2,1)} %param.30) | copy-start | bytes 2654212
  235.5 40.3 %copy-start.2 = (bf16[1,144,3072]{2,1,0:T(8,128)(2,1)S(1)}, bf16[1,144,3072]{2,1,0:T(8,128)(2,1)}, u32[]{:S(2)}) copy-start(bf16[1,144,3072]{2,1,0:T(8,128)(2,1)} %param.29) | copy-start | bytes 2654212
  235.6 40.3 %copy-start.8 = (f32[3072]{0:T(1024)S(1)}, f32[3072]{0:T(1024)}, u32[]{:S(2)}) copy-start(f32[3072]{0:T(1024)} %param.31) | copy-start | bytes 36868
  240.7 38.7 %copy-start.13 = (f32[3072]{0:T(1024)S(1)}, f32[3072]{0:T(1024)}, u32[]{:S(2)}) copy-start(f32[3072]{0:T(1024)} %param.32) | copy-start | bytes 36868
  240.7 38.7 %copy-start.14 = (f32[64]{0:T(128)S(1)}, f32[64]{0:T(128)}, u32[]{:S(2)}) copy-start(f32[64]{0:T(128)} %param.35) | copy-start | bytes 772
  275.8 3.6 %copy-start.3 = (bf16[144,3072]{1,0:T(8,128)(2,1)S(1)}, bf16[144,3072]{1,0:T(8,128)(2,1)}, u32[]{:S(2)}) copy-start(bf16[144,3072]{1,0:T(8,128)(2,1)} %all-reduce.2.cloned.1.call-done) | copy-start | bytes 2654212
  277.6 2.6 copy-start.6
  (2 other events, 2.7 us)
Sparse Core Ops, SparseCore 0:
  17.4 87.9 all-gather.2
  107.2 89.2 all-gather.4
  240.8 34.9 all-reduce.1
where the time goes:
time: 288 us; the launch traced here: 287 us
  waiting for transfers between devices  200 us (69%)
  matrix products  39.8 us (14%)
  between operations  21.5 us (7%)
  other arithmetic  16.5 us (6%)
  local copies, waits for them, and re-layouts  8.54 us (3%)
    all_gather x1, waiting for transfers between devices, shards(): piece_values = lax.all_gather(block_values, 'tile', axis=0, tiled=True)  91 us
    all_gather x1, waiting for transfers between devices, shards(): piece_keys = lax.all_gather(block_keys, 'tile', axis=0, tiled=True)  76.1 us
    psum x1, waiting for transfers between devices, shards(): lax.psum(jnp.dot(result, out_weight, preferred_element_type=jnp.float32)....  33.1 us
    dot_general x4, matrix products, attend_block(): jnp.einsum('hqd,khd->hqk', query_block, piece_keys, preferred_element_typ...  25.6 us
    dot_general x4, matrix products, attend_block(): jnp.einsum('hqk,khd->hqd', weights.astype(jnp.bfloat16), piece_values, pr...  8.29 us
  transfers between devices with their start and end apart: 3, of which 3 were waited for; matrix products, arithmetic and copies ran while one was open for 2% of the time, Pallas kernels for 0%

commit v1 on v0

--- a/solution.py
+++ b/solution.py
@@ -178,8 +178,12 @@
     safe_total = jnp.where(totals > 0, totals, 1.0)
     result = jnp.where(totals[..., None] > 0, blended / safe_total[..., None], 0.0)
     result = result.transpose(1, 0, 2).reshape(pixels, feature_width).astype(jnp.bfloat16)
-    projected = lax.psum(
-        jnp.dot(result, out_weight, preferred_element_type=jnp.float32).astype(jnp.bfloat16), "tp"
+    projected = jnp.sum(
+        lax.all_gather(
+            jnp.dot(result, out_weight, preferred_element_type=jnp.float32).astype(jnp.bfloat16),
+            "tp",
+        ),
+        axis=0,
     ).astype(jnp.float32)
     state = hidden.reshape(pixels, model_width).astype(jnp.float32) + gate * (
         projected + mlp_term.reshape(pixels, model_width).astype(jnp.float32)

time: 288 us -> 272 us (0.944)
  waiting for transfers between devices: 200 us -> 185 us
    psum x1 -> x0, waiting for transfers between devices: 33.1 us -> none  [shards(): lax.psum(jnp.dot(result, out_weight, preferred_element_type=jnp.float32)....]
    all_gather x0 -> x1, waiting for transfers between devices: none -> 18.2 us  [shards(): lax.all_gather(jnp.dot(result, out_weight, preferred_element_type=jnp.flo...]
where the time goes in v1:
time: 272 us; the launch traced here: 271 us
  waiting for transfers between devices  185 us (68%)
  matrix products  39.7 us (15%)
  between operations  21.5 us (8%)
  other arithmetic  16.1 us (6%)
  local copies, waits for them, and re-layouts  8.54 us (3%)
    all_gather x1, waiting for transfers between devices, shards(): piece_values = lax.all_gather(block_values, 'tile', axis=0, tiled=True)  90.3 us
    all_gather x1, waiting for transfers between devices, shards(): piece_keys = lax.all_gather(block_keys, 'tile', axis=0, tiled=True)  76.3 us
    dot_general x4, matrix products, attend_block(): jnp.einsum('hqd,khd->hqk', query_block, piece_keys, preferred_element_typ...  25.6 us
    all_gather x1, waiting for transfers between devices, shards(): lax.all_gather(jnp.dot(result, out_weight, preferred_element_type=jnp.flo...  18.2 us
    dot_general x4, matrix products, attend_block(): jnp.einsum('hqk,khd->hqd', weights.astype(jnp.bfloat16), piece_values, pr...  8.29 us
  transfers between devices with their start and end apart: 3, of which 3 were waited for; matrix products, arithmetic and copies ran while one was open for 2% of the time, Pallas kernels for 0%

profile of v1, /device:TPU:1, one launch (start us, length us, event | category | flops | bytes accessed | tf_op | source)
XLA Modules:
  0.0 271.5 jit_solution(8416174788711759358)
XLA Ops:
  7.3 1.4 copy.81
  8.8 1.0 multiply_reduce_fusion.1
  12.7 1.0 copy.57
  16.0 1.2 copy.63
  19.4 1.9 fusion.131
  21.4 1.3 compare_and_fusion
  27.9 1.3 fusion.121
  29.3 76.3 %all-gather.5.cloned.1.call-done = bf16[2816,8,128]{2,1,0:T(8,128)(2,1)} async-done(((bf16[176,8,128]{2,1,0:T(8,128)(2,1)}), bf16[2816,8,128]{2,1,0:T(8,128)(2,1)}) %all-gather.5.cloned.1.call-update) | async-done | bytes 5767184 | tf_op jit(solution)/shard_map/all_gather | solution.py:139
  105.7 90.3 %all-gather.7.cloned.1.call-done = bf16[2816,8,128]{2,1,0:T(8,128)(2,1)} async-done(((bf16[176,8,128]{2,1,0:T(8,128)(2,1)}), bf16[2816,8,128]{2,1,0:T(8,128)(2,1)}) %all-gather.7.cloned.1.call-update) | async-done | bytes 5767184 | tf_op jit(solution)/shard_map/all_gather | solution.py:140
  196.0 9.6 %conditional.4 = (f32[8,36,128]{2,1,0:T(8,128)S(1)}, f32[8,36]{1,0:T(8,128)S(1)}) conditional(s32[]{:T(128)} %convert_element_type.125, () %tuple.56, (pred[2816]{0:T(1024)(128)(4,1)S(1)}, bf16[8,144,128]{1,0,2:T(8,128)(2,1)S(1)}, bf16[2816,8,128]{2,1,0:T(8,128)(2,1)}, bf16[2816,8,128]{2,1,0:T(8,128)(2,1)}) %tuple.113), branch_computations={%region_5.6_spmd, %region_6.9_spmd} | conditional | flops 420951456 | bytes 39402944 | solution.py:89
  196.4 6.4 %fusion.132 = (f32[8,36]{1,0:T(8,128)S(1)}, f32[8,36,2816]{2,1,0:T(8,128)S(1)}) fusion(bf16[2816,8,128]{2,1,0:T(8,128)(2,1)} %get-tuple-element.112, bf16[8,144,128]{2,1,0:T(8,128)(2,1)S(1)} %copy.64, pred[2816]{0:T(1024)(128)(4,1)S(1)} %get-tuple-element.44), kind=kOutput, calls=%fused_computation.174 | convolution fusion | flops 210050784 | bytes 9097344 | tf_op jit(solution)/shard_map/cond/branch_1_fun/hqd,khd->hqk/dot_general | solution.py:63
  203.5 2.1 fusion.14
  205.6 9.8 %conditional.5 = (f32[8,36,128]{2,1,0:T(8,128)S(1)}, f32[8,36]{1,0:T(8,128)S(1)}) conditional(s32[]{:T(128)} %convert_element_type.140, () %tuple.58, (pred[2816]{0:T(1024)(128)(4,1)S(1)}, bf16[8,144,128]{1,0,2:T(8,128)(2,1)S(1)}, bf16[2816,8,128]{2,1,0:T(8,128)(2,1)}, bf16[2816,8,128]{2,1,0:T(8,128)(2,1)}) %tuple.114), branch_computations={%region_10.11_spmd, %region_11.14_spmd} | conditional | flops 420951456 | bytes 39402944 | solution.py:89
  206.2 6.4 %fusion.133 = (f32[8,36]{1,0:T(8,128)S(1)}, f32[8,36,2816]{2,1,0:T(8,128)S(1)}) fusion(bf16[2816,8,128]{2,1,0:T(8,128)(2,1)} %get-tuple-element.116, bf16[8,144,128]{2,1,0:T(8,128)(2,1)S(1)} %copy.67, pred[2816]{0:T(1024)(128)(4,1)S(1)} %get-tuple-element.48), kind=kOutput, calls=%fused_computation.175 | convolution fusion | flops 210050784 | bytes 9097344 | tf_op jit(solution)/shard_map/cond/branch_1_fun/hqd,khd->hqk/dot_general | solution.py:63
  213.3 2.1 fusion.35
  215.4 9.6 %conditional.6 = (f32[8,36,128]{2,1,0:T(8,128)S(1)}, f32[8,36]{1,0:T(8,128)S(1)}) conditional(s32[]{:T(128)} %convert_element_type.141, () %tuple.59, (pred[2816]{0:T(1024)(128)(4,1)S(1)}, bf16[8,144,128]{1,0,2:T(8,128)(2,1)S(1)}, bf16[2816,8,128]{2,1,0:T(8,128)(2,1)}, bf16[2816,8,128]{2,1,0:T(8,128)(2,1)}) %tuple.115), branch_computations={%region_15.16_spmd, %region_16.19_spmd} | conditional | flops 420951456 | bytes 39402944 | solution.py:89
  215.8 6.4 %fusion.134 = (f32[8,36]{1,0:T(8,128)S(1)}, f32[8,36,2816]{2,1,0:T(8,128)S(1)}) fusion(bf16[2816,8,128]{2,1,0:T(8,128)(2,1)} %get-tuple-element.120, bf16[8,144,128]{2,1,0:T(8,128)(2,1)S(1)} %copy.70, pred[2816]{0:T(1024)(128)(4,1)S(1)} %get-tuple-element.52), kind=kOutput, calls=%fused_computation.176 | convolution fusion | flops 210050784 | bytes 9097344 | tf_op jit(solution)/shard_map/cond/branch_1_fun/hqd,khd->hqk/dot_general | solution.py:63
  222.9 2.1 fusion.56
  225.0 9.8 %conditional.7 = (f32[8,36,128]{2,1,0:T(8,128)S(1)}, f32[8,36]{1,0:T(8,128)S(1)}) conditional(s32[]{:T(128)} %convert_element_type.142, () %tuple.60, (pred[2816]{0:T(1024)(128)(4,1)S(1)}, bf16[8,144,128]{1,0,2:T(8,128)(2,1)S(1)}, bf16[2816,8,128]{2,1,0:T(8,128)(2,1)}, bf16[2816,8,128]{2,1,0:T(8,128)(2,1)}) %tuple.116), branch_computations={%region_20.21_spmd, %region_21.24_spmd} | conditional | flops 420951456 | bytes 39402944 | solution.py:89
  225.7 6.4 %fusion.135 = (f32[8,36]{1,0:T(8,128)S(1)}, f32[8,36,2816]{2,1,0:T(8,128)S(1)}) fusion(bf16[2816,8,128]{2,1,0:T(8,128)(2,1)} %get-tuple-element.124, bf16[8,144,128]{2,1,0:T(8,128)(2,1)S(1)} %copy.73, pred[2816]{0:T(1024)(128)(4,1)S(1)} %get-tuple-element.56), kind=kOutput, calls=%fused_computation.177 | convolution fusion | flops 210050784 | bytes 9097344 | tf_op jit(solution)/shard_map/cond/branch_1_fun/hqd,khd->hqk/dot_general | solution.py:63
  232.8 2.1 fusion.77
  235.0 5.0 %convolution_convert_fusion = bf16[144,3072]{1,0:T(8,128)(2,1)} fusion(bf16[1024,3072]{1,0:T(8,128)(2,1)} %param.28, f32[8,144]{1,0:T(8,128)S(1)} %broadcast_select_fusion, f32[8,36,128]{2,1,0:T(8,128)S(1)} %get-tuple-element.77, f32[8,36,128]{2,1,0:T(8,128)S(1)} %get-tuple-element.76, f32[8,36,128]{2,1,0:T(8,128)S(1)} %get-tuple-element.75, ...), kind=kOutput, calls=%fused_computation.60 | convolution fusion | flops 907296768 | bytes 7771776 | tf_op jit(solution)/shard_map/dot_general | solution.py:183
  242.3 18.2 %all-gather.9.cloned.1.call-done = bf16[288,3072]{1,0:T(8,128)(2,1)} async-done(((bf16[144,3072]{1,0:T(8,128)(2,1)}), bf16[288,3072]{1,0:T(8,128)(2,1)}) %all-gather.9.cloned.1.call-update) | async-done | bytes 1769488 | tf_op jit(solution)/shard_map/all_gather | solution.py:182
  260.4 1.9 reduce_sum.96
  (110 shorter events, 14.6 us)
Async XLA Ops:
  7.2 256.3 %copy-start = (bf16[3072,64]{0,1:T(8,128)(2,1)S(1)}, bf16[3072,64]{0,1:T(8,128)(2,1)}, u32[]{:S(2)}) copy-start(bf16[3072,64]{0,1:T(8,128)(2,1)} %param.34) | copy-start | bytes 1179652
  7.2 2.6 copy-start.4
  7.2 98.5 %all-gather.5.cloned.1.call-start = ((), (), s32[]{:S(2)}) async-start(), calls=%async_computation | async-start | bytes 6127616 | tf_op jit(solution)/shard_map/all_gather | solution.py:139
  8.7 4.9 %copy-start.10 = (f32[128]{0:T(128)S(1)}, f32[128]{0:T(128)}, u32[]{:S(2)}) copy-start(f32[128]{0:T(128)} %param.27) | copy-start | bytes 1540
  8.7 5.1 %copy-start.11 = (f32[128]{0:T(128)S(1)}, f32[128]{0:T(128)}, u32[]{:S(2)}) copy-start(f32[128]{0:T(128)} %param.26) | copy-start | bytes 1540
  15.3 2.0 copy-start.3
  15.3 3.5 %copy-start.9 = (s32[2]{0:T(128)S(1)}, s32[2]{0:T(128)}, u32[]{:S(2)}) copy-start(s32[2]{0:T(128)} %param.37) | copy-start | bytes 28
  17.3 178.7 %all-gather.7.cloned.1.call-start = ((), (), s32[]{:S(2)}) async-start(), calls=%async_computation.1 | async-start | bytes 6127616 | tf_op jit(solution)/shard_map/all_gather | solution.py:140
  18.1 242.3 %all-gather.9.cloned.1.call-start = ((), (), s32[]{:S(2)}) async-start(), calls=%async_computation.2 | async-start | bytes 2654208 | tf_op jit(solution)/shard_map/all_gather | solution.py:182
  196.4 7.1 %slice-start = ((s8[5767168]{0:T(1024)(128)(4,1)}), s8[4194304]{0:T(1024)(128)(4,1)S(1)}, s32[]{:S(2)}) async-start(s8[5767168]{0:T(1024)(128)(4,1)} %bitcast.72), calls=%async_computation.3 | async-start | bytes 8388608 | tf_op jit(solution)/shard_map/cond
  196.4 7.1 %slice-start.1 = ((s8[5767168]{0:T(1024)(128)(4,1)}), s8[1572864]{0:T(1024)(128)(4,1)S(1)}, s32[]{:S(2)}) async-start(s8[5767168]{0:T(1024)(128)(4,1)} %bitcast.72), calls=%async_computation.4 | async-start | bytes 3145728 | tf_op jit(solution)/shard_map/cond
  206.2 7.1 %slice-start.2 = ((s8[5767168]{0:T(1024)(128)(4,1)}), s8[4194304]{0:T(1024)(128)(4,1)S(1)}, s32[]{:S(2)}) async-start(s8[5767168]{0:T(1024)(128)(4,1)} %bitcast.74), calls=%async_computation.5 | async-start | bytes 8388608 | tf_op jit(solution)/shard_map/cond
  206.2 7.1 %slice-start.3 = ((s8[5767168]{0:T(1024)(128)(4,1)}), s8[1572864]{0:T(1024)(128)(4,1)S(1)}, s32[]{:S(2)}) async-start(s8[5767168]{0:T(1024)(128)(4,1)} %bitcast.74), calls=%async_computation.6 | async-start | bytes 3145728 | tf_op jit(solution)/shard_map/cond
  215.8 7.1 %slice-start.4 = ((s8[5767168]{0:T(1024)(128)(4,1)}), s8[4194304]{0:T(1024)(128)(4,1)S(1)}, s32[]{:S(2)}) async-start(s8[5767168]{0:T(1024)(128)(4,1)} %bitcast.76), calls=%async_computation.7 | async-start | bytes 8388608 | tf_op jit(solution)/shard_map/cond
  215.8 7.1 %slice-start.5 = ((s8[5767168]{0:T(1024)(128)(4,1)}), s8[1572864]{0:T(1024)(128)(4,1)S(1)}, s32[]{:S(2)}) async-start(s8[5767168]{0:T(1024)(128)(4,1)} %bitcast.76), calls=%async_computation.8 | async-start | bytes 3145728 | tf_op jit(solution)/shard_map/cond
  225.7 7.1 %slice-start.6 = ((s8[5767168]{0:T(1024)(128)(4,1)}), s8[4194304]{0:T(1024)(128)(4,1)S(1)}, s32[]{:S(2)}) async-start(s8[5767168]{0:T(1024)(128)(4,1)} %bitcast.78), calls=%async_computation.9 | async-start | bytes 8388608 | tf_op jit(solution)/shard_map/cond
  225.7 7.1 %slice-start.7 = ((s8[5767168]{0:T(1024)(128)(4,1)}), s8[1572864]{0:T(1024)(128)(4,1)S(1)}, s32[]{:S(2)}) async-start(s8[5767168]{0:T(1024)(128)(4,1)} %bitcast.78), calls=%async_computation.10 | async-start | bytes 3145728 | tf_op jit(solution)/shard_map/cond
  235.0 7.2 %copy-start.8 = (f32[3072]{0:T(1024)S(1)}, f32[3072]{0:T(1024)}, u32[]{:S(2)}) copy-start(f32[3072]{0:T(1024)} %param.33) | copy-start | bytes 36868
  240.0 22.3 %copy-start.1 = (bf16[1,144,3072]{2,1,0:T(8,128)(2,1)S(1)}, bf16[1,144,3072]{2,1,0:T(8,128)(2,1)}, u32[]{:S(2)}) copy-start(bf16[1,144,3072]{2,1,0:T(8,128)(2,1)} %param.30) | copy-start | bytes 2654212
  240.0 22.3 %copy-start.2 = (bf16[1,144,3072]{2,1,0:T(8,128)(2,1)S(1)}, bf16[1,144,3072]{2,1,0:T(8,128)(2,1)}, u32[]{:S(2)}) copy-start(bf16[1,144,3072]{2,1,0:T(8,128)(2,1)} %param.29) | copy-start | bytes 2654212
  240.0 22.3 %copy-start.7 = (f32[3072]{0:T(1024)S(1)}, f32[3072]{0:T(1024)}, u32[]{:S(2)}) copy-start(f32[3072]{0:T(1024)} %param.31) | copy-start | bytes 36868
  260.4 3.1 %copy-start.12 = (f32[3072]{0:T(1024)S(1)}, f32[3072]{0:T(1024)}, u32[]{:S(2)}) copy-start(f32[3072]{0:T(1024)} %param.32) | copy-start | bytes 36868
  260.4 3.1 %copy-start.13 = (f32[64]{0:T(128)S(1)}, f32[64]{0:T(128)}, u32[]{:S(2)}) copy-start(f32[64]{0:T(128)} %param.35) | copy-start | bytes 772
  262.9 1.4 copy-start.5
  (1 other events, 0.7 us)
Sparse Core Ops, SparseCore 0:
  17.4 88.2 all-gather.4
  107.5 88.4 all-gather.6
  240.2 20.1 all-gather.8
